TPU v7x, 32 devices: a whole 2x2x4 slice. The times are simulated.
32 devices in a mesh: gx: 2 (over x), gy: 4 (over y, core), gz: 4 (over z).
Axes of the slice: x: 2, y: 2, z: 4, core: 2. Of those that a mesh axis runs over, the one named last changes fastest.
Arguments:
- solution_in: float32 [16, 128, 512], P('gx', 'gy', 'gz'), may hold values from -6 to 6
- residual_in: float32 [16, 128, 512], P('gx', 'gy', 'gz'), may hold values from -12 to 12
- direction_in: float32 [16, 128, 512], P('gx', 'gy', 'gz'), may hold values from -6 to 6
- material: int32 [16, 128, 512], P('gx', 'gy', 'gz'), may hold values from 0 to 7
- cond_table: float32 [8], replicated, may hold values from 0.5 to 4
- cap_table: float32 [8], replicated, may hold values from 0.2 to 1
- gas_flux: float32 [128, 512], P('gy', 'gz'), may hold values from -6 to 6
- supply_map: int32 [128, 512], P('gy', 'gz'), may hold values from 0 to 511, as said below
Outputs:
- solution: float32 [16, 128, 512], P('gx', 'gy', 'gz')
- residual: float32 [16, 128, 512], P('gx', 'gy', 'gz')
- direction: float32 [16, 128, 512], P('gx', 'gy', 'gz')
Inputs may be any that keep to these rules, and one draw needn't show every extreme that they name: `supply_map`: the gas faces are laid out so that the faces held by index q of gz, in their slots t * 128 / 4 to (t + 1) * 128 / 4 - 1, supply solid faces held by index t of gz in the same row; every gas face supplies exactly one solid face of its row.
All inputs are finite; a program needn't handle non-finite values.
Results may differ from a plain program's by a relative error of at most 0.0006.
Values sent between devices are 32-bit elements; how exact they have to be, the bound alone decides.
A program may use at most 64 MiB of HBM per device.

v0:
```python
import jax
import jax.numpy as jnp
from jax import lax
from jax.sharding import PartitionSpec as P

STEPS = 4


def extended(block, sides, width):
    for axis, dim in sides:
        count = lax.axis_size(axis)
        forward = [(i, i + 1) for i in range(count - 1)]
        backward = [(target, source) for source, target in forward]
        low = lax.ppermute(
            lax.slice_in_dim(block, block.shape[dim] - width, None, axis=dim), axis, forward
        )
        high = lax.ppermute(lax.slice_in_dim(block, 0, width, axis=dim), axis, backward)
        block = jnp.concatenate([low, block, high], axis=dim)
    return block


def harmonic(lower_side, upper_side):
    return (
        2.0
        * lower_side
        * upper_side
        / (jnp.where(lower_side > 0, lower_side, 1.0) + jnp.where(upper_side > 0, upper_side, 1.0))
    )


def face_terms(cond):
    return (
        harmonic(cond[:-1], cond[1:]),
        harmonic(cond[:, :-1], cond[:, 1:]),
        harmonic(cond[:, :, :-1], cond[:, :, 1:]),
    )


def operate(values, capacity, conductance):
    result = capacity * values
    face_flow = conductance[0] * (values[1:] - values[:-1])
    result = (
        result
        - jnp.pad(face_flow, ((0, 1), (0, 0), (0, 0)))
        + jnp.pad(face_flow, ((1, 0), (0, 0), (0, 0)))
    )
    face_flow = conductance[1] * (values[:, 1:] - values[:, :-1])
    result = (
        result
        - jnp.pad(face_flow, ((0, 0), (0, 1), (0, 0)))
        + jnp.pad(face_flow, ((0, 0), (1, 0), (0, 0)))
    )
    face_flow = conductance[2] * (values[:, :, 1:] - values[:, :, :-1])
    result = (
        result
        - jnp.pad(face_flow, ((0, 0), (0, 0), (0, 1)))
        + jnp.pad(face_flow, ((0, 0), (0, 0), (1, 0)))
    )
    return result


def lookup_code(codes, table):
    summed = jnp.zeros(codes.shape, jnp.float32)
    for material_id in range(table.shape[0]):
        summed = summed + jnp.where(
            codes == jnp.float32(material_id + 1), table[material_id], jnp.float32(0.0)
        )
    return summed


def spectrum(cond_table, cap_table):
    lowest = jnp.min(cap_table)
    highest = jnp.max(cap_table) + 12.0 * jnp.max(cond_table)
    return (0.5 * (highest + lowest), 0.5 * (highest - lowest))


def next_term(applied, terms, center, half_width):
    shifted = (applied - center * terms[-1]) / half_width
    if len(terms) == 1:
        return shifted
    return 2.0 * shifted - terms[-2]


def shift_matrix(center, half_width, steps):
    dimension = 2 * steps + 1
    matrix = jnp.zeros((dimension, dimension), jnp.float32)
    for offset, length in ((0, steps + 1), (steps + 1, steps)):
        for column in range(length - 1):
            matrix = matrix.at[offset + column, offset + column].set(center)
            matrix = matrix.at[offset + column + 1, offset + column].set(
                half_width if column == 0 else 0.5 * half_width
            )
            if column >= 1:
                matrix = matrix.at[offset + column - 1, offset + column].set(0.5 * half_width)
    return matrix


def coefficients(gram, center, half_width, steps):
    dimension = 2 * steps + 1
    matrix = shift_matrix(center, half_width, steps)
    highest_prec = lax.Precision.HIGHEST

    def gram_product(first_vec, second_vec):
        return jnp.dot(
            first_vec, jnp.dot(gram, second_vec, precision=highest_prec), precision=highest_prec
        )

    direct = jnp.zeros((dimension,), jnp.float32).at[0].set(1.0)
    residue = jnp.zeros((dimension,), jnp.float32).at[steps + 1].set(1.0)
    moved = jnp.zeros((dimension,), jnp.float32)
    norm_now = gram_product(residue, residue)
    for sweep in range(steps):
        mapped = jnp.dot(matrix, direct, precision=highest_prec)
        step_length = norm_now / gram_product(direct, mapped)
        moved = moved + step_length * direct
        residue = residue - step_length * mapped
        norm_next = gram_product(residue, residue)
        direct = residue + norm_next / norm_now * direct
        norm_now = norm_next
    return (moved, residue, direct)


def combine(weights, basis):
    summed = weights[0] * basis[0]
    for position in range(1, len(basis)):
        summed = summed + weights[position] * basis[position]
    return summed


def inside(values, depth):
    return values[depth:-depth, depth:-depth, depth:-depth]


def body(
    solution_in, residual_in, direction_in, material, cond_table, cap_table, gas_flux, supply_map
):
    surface_rows, surface_width = gas_flux.shape
    groups = lax.axis_size("gz")
    segment = surface_width // groups
    arrived = lax.all_to_all(
        gas_flux.reshape(surface_rows, groups, segment),
        "gz",
        split_axis=1,
        concat_axis=1,
        tiled=True,
    )
    arrived = arrived.reshape(surface_rows, surface_width)
    slot = (
        supply_map // surface_width * segment
        + supply_map % surface_width
        - lax.axis_index("gz") * segment
    )
    incoming = jnp.take_along_axis(arrived, slot, axis=1)
    is_top = lax.axis_index("gx") == lax.axis_size("gx") - 1
    start = residual_in.at[-1].add(jnp.where(is_top, incoming, jnp.float32(0.0)))
    codes = (material + 1).astype(jnp.float32)
    center, half_width = spectrum(cond_table, cap_table)
    first = extended(jnp.stack([direction_in, start, codes]), (("gx", 1), ("gy", 2), ("gz", 3)), 1)
    conductance = face_terms(lookup_code(first[2], cond_table))
    capacity_ext = lookup_code(first[2], cap_table)
    dir_terms = [direction_in]
    res_terms = [start]
    dir_applied = inside(operate(first[0], capacity_ext, conductance), 1)
    res_applied = inside(operate(first[1], capacity_ext, conductance), 1)
    res_terms.append(next_term(res_applied, res_terms, center, half_width))
    dir_terms.append(next_term(dir_applied, dir_terms, center, half_width))
    for sweep in range(1, STEPS):
        if sweep < STEPS - 1:
            layered = extended(
                jnp.stack([dir_terms[-1], res_terms[-1]]), (("gx", 1), ("gy", 2), ("gz", 3)), 1
            )
            dir_applied = inside(operate(layered[0], capacity_ext, conductance), 1)
            res_applied = inside(operate(layered[1], capacity_ext, conductance), 1)
            res_terms.append(next_term(res_applied, res_terms, center, half_width))
        else:
            layered = extended(dir_terms[-1], (("gx", 0), ("gy", 1), ("gz", 2)), 1)
            dir_applied = inside(operate(layered, capacity_ext, conductance), 1)
        dir_terms.append(next_term(dir_applied, dir_terms, center, half_width))
    basis = dir_terms + res_terms
    stacked = jnp.stack([term.reshape(-1) for term in basis])
    partial_gram = jnp.dot(stacked, stacked.T, precision=lax.Precision.HIGHEST)
    gram = lax.psum(partial_gram, ("gx", "gy", "gz"))
    moved, residue, direct = coefficients(gram, center, half_width, STEPS)
    return (solution_in + combine(moved, basis), combine(residue, basis), combine(direct, basis))


def solution(mesh):
    in_specs = (
        P("gx", "gy", "gz"),
        P("gx", "gy", "gz"),
        P("gx", "gy", "gz"),
        P("gx", "gy", "gz"),
        P(),
        P(),
        P("gy", "gz"),
        P("gy", "gz"),
    )
    out_specs = (P("gx", "gy", "gz"), P("gx", "gy", "gz"), P("gx", "gy", "gz"))
    return jax.shard_map(body, mesh=mesh, in_specs=in_specs, out_specs=out_specs, check_vma=False)
```

profile of v0, /device:TPU:0, one launch (start us, length us, event | category | flops | bytes accessed | tf_op | source)
XLA Modules:
  0.0 260.0 jit_solution(15775123754584945129)
XLA Ops:
  2.2 6.3 %all-to-all-start = ((f32[4,1,1024]{2,1,0:T(1,128)}), f32[4,1,1024]{2,1,0:T(1,128)S(1)}, u32[]{:S(2)}, u32[]{:S(2)}) async-start(f32[4,1,1024]{2,1,0:T(1,128)} %reshape.745), calls=%async_computation | async-start | bytes 32768 | tf_op jit(solution)/shard_map/all_to_all | solution.py:140
  10.2 3.9 %all-to-all-done = f32[4,1,1024]{2,1,0:T(1,128)S(1)} async-done(((f32[4,1,1024]{2,1,0:T(1,128)}), f32[4,1,1024]{2,1,0:T(1,128)S(1)}, u32[]{:S(2)}, u32[]{:S(2)}) %all-to-all-start) | async-done | bytes 16416 | tf_op jit(solution)/shard_map/all_to_all | solution.py:140
  15.6 25.6 %gather_fusion = f32[4096]{0:T(1024)S(1)} fusion(f32[32,128]{1,0:T(8,128)S(1)} %reshape.660, s32[4096]{0:T(1024)S(1)} %fusion.80), kind=kCustom, calls=%fused_computation | custom fusion | bytes 65536 | tf_op jit(solution)/shard_map/jit(take_along_axis)/gather | solution.py:153
  41.3 3.4 %collective-permute-start = (f32[3,1,32,128]{3,2,1,0:T(8,128)S(1)}, f32[3,1,32,128]{3,2,1,0:T(8,128)S(1)}, u32[]{:S(2)}, u32[]{:S(2)}) collective-permute-start(f32[3,1,32,128]{3,2,1,0:T(8,128)S(1)} %get-tuple-element.320), channel_id=1, source_target_pairs={{0,16},{1,17},{2,18},{3,19},{4,20},{5,21},{6,22},{7,23},{8,24},{9,... | collective-permute-start | bytes 147464 | tf_op jit(solution)/shard_map/ppermute | solution.py:14
  46.7 4.0 %collective-permute-done.1 = f32[3,1,32,128]{3,2,1,0:T(8,128)S(1)} collective-permute-done((f32[3,1,32,128]{3,2,1,0:T(8,128)S(1)}, f32[3,1,32,128]{3,2,1,0:T(8,128)S(1)}, u32[]{:S(2)}, u32[]{:S(2)}) %collective-permute-start.1) | collective-permute-done | bytes 49184 | tf_op jit(solution)/shard_map/ppermute | solution.py:17
  54.0 2.8 %collective-permute-done.3 = f32[3,10,1,128]{3,2,1,0:T(1,128)S(1)} collective-permute-done((f32[3,10,1,128]{3,2,1,0:T(1,128)S(1)}, f32[3,10,1,128]{3,2,1,0:T(1,128)S(1)}, u32[]{:S(2)}, u32[]{:S(2)}) %collective-permute-start.3) | collective-permute-done | bytes 15392 | tf_op jit(solution)/shard_map/ppermute | solution.py:17
  57.4 2.6 collective-permute-start.4
  67.0 5.8 %bitcast_multiply_fusion.6 = (f32[10,34,130]{2,1,0:T(8,128)S(1)}, f32[1,10,34,130]{3,2,1,0:T(8,128)S(1)}, pred[1,10,34,130]{3,2,1,0:T(8,128)(4,1)S(1)}, pred[1,1...) fusion(f32[3,10,34,130]{3,2,1,0:T(8,128)S(1)} %pad_maximum_fusi, ...), kind=kLoop, calls=%fused_computation.85 | loop fusion | flops 1060800 | bytes 1060832 | tf_op jit(solution)/shard_map/mul | solution.py:40
  72.8 5.4 %add_add_fusion = f32[1,10,34,130]{3,2,1,0:T(8,128)S(1)} fusion(pred[1,10,34,130]{3,2,1,0:T(8,128)(4,1)S(1)} %get-tuple-element.283, pred[1,10,34,130]{3,2,1,0:T(8,128)(4,1)S(1)} %get-tuple-element.282, pred[1,10,34,130]{3,2,1,0:T(8,128)(4,1)S(1)} %get-tuple-element.281, pred[1,10,34,130]{3,2,1,0:T(8,128)(4,1)S(1)} %get-tuple-element.280, ...), kind=kLoop, calls=%fused_computation.86 | loop fusion | flops 663000 | bytes 530432 | tf_op jit(solution)/shard_map/add | solution.py:65
  82.8 4.2 %collective-permute-done.7 = f32[2,1,32,128]{3,2,1,0:T(8,128)S(1)} collective-permute-done((f32[2,1,32,128]{3,2,1,0:T(8,128)S(1)}, f32[2,1,32,128]{3,2,1,0:T(8,128)S(1)}, u32[]{:S(2)}, u32[]{:S(2)}) %collective-permute-start.7) | collective-permute-done | bytes 32800 | tf_op jit(solution)/shard_map/ppermute | solution.py:17
  87.1 2.4 collective-permute-start.8
  90.8 3.3 %collective-permute-done.9 = f32[2,10,1,128]{3,2,1,0:T(1,128)S(1)} collective-permute-done((f32[2,10,1,128]{3,2,1,0:T(1,128)S(1)}, f32[2,10,1,128]{3,2,1,0:T(1,128)S(1)}, u32[]{:S(2)}, u32[]{:S(2)}) %collective-permute-start.9) | collective-permute-done | bytes 10272 | tf_op jit(solution)/shard_map/ppermute | solution.py:17
  94.3 4.3 %collective-permute-start.10 = (f32[2,10,34,1]{3,2,1,0:T(8,128)S(1)}, f32[2,10,34,1]{3,2,1,0:T(8,128)S(1)}, u32[]{:S(2)}, u32[]{:S(2)}) collective-permute-start(f32[2,10,34,1]{3,2,1,0:T(8,128)S(1)} %get-tuple-element.318), channel_id=1, source_target_pairs={{0,1},{1,2},{2,3},{4,5},{5,6},{6,7},{8,9},{9,10},{10,11},{12,13},{... | collective-permute-start | bytes 8168 | tf_op jit(solution)/shard_map/ppermute | solution.py:14
  99.9 7.0 %collective-permute-done.10 = f32[2,10,34,1]{3,2,1,0:T(8,128)S(1)} collective-permute-done((f32[2,10,34,1]{3,2,1,0:T(8,128)S(1)}, f32[2,10,34,1]{3,2,1,0:T(8,128)S(1)}, u32[]{:S(2)}, u32[]{:S(2)}) %collective-permute-start.10) | collective-permute-done | bytes 2752 | tf_op jit(solution)/shard_map/ppermute | solution.py:14
  106.9 4.7 %collective-permute-done.11 = f32[2,10,34,1]{3,2,1,0:T(8,128)S(1)} collective-permute-done((f32[2,10,34,1]{3,2,1,0:T(8,128)S(1)}, f32[2,10,34,1]{3,2,1,0:T(8,128)S(1)}, u32[]{:S(2)}, u32[]{:S(2)}) %collective-permute-start.11) | collective-permute-done | bytes 2752 | tf_op jit(solution)/shard_map/ppermute | solution.py:17
  116.7 4.2 %collective-permute-done.13 = f32[2,1,32,128]{3,2,1,0:T(8,128)S(1)} collective-permute-done((f32[2,1,32,128]{3,2,1,0:T(8,128)S(1)}, f32[2,1,32,128]{3,2,1,0:T(8,128)S(1)}, u32[]{:S(2)}, u32[]{:S(2)}) %collective-permute-start.13) | collective-permute-done | bytes 32800 | tf_op jit(solution)/shard_map/ppermute | solution.py:17
  120.9 1.8 collective-permute-start.14
  124.0 1.9 collective-permute-done.15
  126.2 2.4 collective-permute-start.16
  129.9 7.0 %collective-permute-done.16 = f32[2,10,34,1]{3,2,1,0:T(8,128)S(1)} collective-permute-done((f32[2,10,34,1]{3,2,1,0:T(8,128)S(1)}, f32[2,10,34,1]{3,2,1,0:T(8,128)S(1)}, u32[]{:S(2)}, u32[]{:S(2)}) %collective-permute-start.16) | collective-permute-done | bytes 2752 | tf_op jit(solution)/shard_map/ppermute | solution.py:14
  136.9 4.7 %collective-permute-done.17 = f32[2,10,34,1]{3,2,1,0:T(8,128)S(1)} collective-permute-done((f32[2,10,34,1]{3,2,1,0:T(8,128)S(1)}, f32[2,10,34,1]{3,2,1,0:T(8,128)S(1)}, u32[]{:S(2)}, u32[]{:S(2)}) %collective-permute-start.17) | collective-permute-done | bytes 2752 | tf_op jit(solution)/shard_map/ppermute | solution.py:17
  147.5 4.2 %collective-permute-done.19 = f32[1,32,128]{2,1,0:T(8,128)S(1)} collective-permute-done((f32[1,32,128]{2,1,0:T(8,128)S(1)}, f32[1,32,128]{2,1,0:T(8,128)S(1)}, u32[]{:S(2)}, u32[]{:S(2)}) %collective-permute-start.19) | collective-permute-done | bytes 16416 | tf_op jit(solution)/shard_map/ppermute | solution.py:17
  156.1 1.9 dynamic-slice.147
  163.1 2.5 collective-permute-start.22
  167.0 3.3 %collective-permute-done.22 = f32[10,34,1]{2,1,0:T(8,128)S(1)} collective-permute-done((f32[10,34,1]{2,1,0:T(8,128)S(1)}, f32[10,34,1]{2,1,0:T(8,128)S(1)}, u32[]{:S(2)}, u32[]{:S(2)}) %collective-permute-start.22) | collective-permute-done | bytes 1392 | tf_op jit(solution)/shard_map/ppermute | solution.py:14
  170.3 4.7 %collective-permute-done.23 = f32[10,34,1]{2,1,0:T(8,128)S(1)} collective-permute-done((f32[10,34,1]{2,1,0:T(8,128)S(1)}, f32[10,34,1]{2,1,0:T(8,128)S(1)}, u32[]{:S(2)}, u32[]{:S(2)}) %collective-permute-start.23) | collective-permute-done | bytes 1392 | tf_op jit(solution)/shard_map/ppermute | solution.py:17
  178.1 1.9 stack.43
  180.0 2.9 %fusion.119 = f32[9,9]{1,0:T(8,128)S(1)} fusion(f32[9,32768]{1,0:T(8,128)S(1)} %stack.43), kind=kOutput, calls=%fused_computation.275 | convolution fusion | flops 31850496 | bytes 1179972 | tf_op jit(solution)/shard_map/dot_general | solution.py:181
  183.0 38.1 %psum.7 = f32[9,9]{1,0:T(8,128)S(1)} all-reduce(f32[9,9]{1,0:T(8,128)S(1)} %fusion.119), channel_id=1, replica_groups=mesh['gx'=2,'gy'=4,'gz'=4] {'gx','gy','gz'}, use_global_device_ids=true, to_apply=%region_3.4 | all-reduce | flops 81 | bytes 648 | tf_op jit(solution)/shard_map/psum | solution.py:182
  240.9 6.2 %multiply_add_fusion = f32[8,32,128]{2,1,0:T(8,128)} fusion(f32[8,32,128]{2,1,0:T(8,128)S(1)} %fusion.54, f32[8,32,128]{2,1,0:T(8,128)S(1)} %fusion.66, f32[8,32,128]{2,1,0:T(8,128)S(1)} %get-tuple-element.383, f32[8,32,128]{2,1,0:T(8,128)S(1)} %fusion.78, f32[8,32,128]{2,1,0:T(8,128)S(1)} %fusion.58, f32[8,32,128]{2,1,0:T(8,128)S(1)} %fusion.62, ...), kind=kLoop, calls=%fused_computation.187 | loop fusion | flops 557056 | bytes 1310756 | tf_op jit(solution)/shard_map/add | solution.py:126
  247.2 6.4 %multiply_add_fusion.1 = f32[8,32,128]{2,1,0:T(8,128)} fusion(f32[8,32,128]{2,1,0:T(8,128)S(1)} %fusion.54, f32[8,32,128]{2,1,0:T(8,128)S(1)} %fusion.66, f32[8,32,128]{2,1,0:T(8,128)S(1)} %get-tuple-element.383, f32[8,32,128]{2,1,0:T(8,128)S(1)} %fusion.78, f32[8,32,128]{2,1,0:T(8,128)S(1)} %fusion.58, f32[8,32,128]{2,1,0:T(8,128)S(1)} %fusion.62, ...), kind=kLoop, calls=%fused_computation.188 | loop fusion | flops 557056 | bytes 1310756 | tf_op jit(solution)/shard_map/add | solution.py:126
  253.6 6.4 %add_add_fusion.2 = f32[8,32,128]{2,1,0:T(8,128)} fusion(f32[8,32,128]{2,1,0:T(8,128)S(1)} %copy-done.3, f32[8,32,128]{2,1,0:T(8,128)S(1)} %fusion.54, f32[8,32,128]{2,1,0:T(8,128)S(1)} %fusion.66, f32[8,32,128]{2,1,0:T(8,128)S(1)} %get-tuple-element.383, f32[8,32,128]{2,1,0:T(8,128)S(1)} %fusion.78, f32[8,32,128]{2,1,0:T(8,128)S(1)} %fusion.58, ...), kind=kLoop, calls=%fused_computation.189 | loop fusion | flops 589824 | bytes 1441828 | tf_op jit(solution)/shard_map/add | solution.py:184
  (161 shorter events, 57.8 us)
Async XLA Ops:
  2.2 11.9 %all-to-all-start = ((f32[4,1,1024]{2,1,0:T(1,128)}), f32[4,1,1024]{2,1,0:T(1,128)S(1)}, u32[]{:S(2)}, u32[]{:S(2)}) async-start(f32[4,1,1024]{2,1,0:T(1,128)} %reshape.745), calls=%async_computation | async-start | bytes 32768 | tf_op jit(solution)/shard_map/all_to_all | solution.py:140
  15.5 25.7 %copy-start = (f32[8,32,128]{2,1,0:T(8,128)S(1)}, f32[8,32,128]{2,1,0:T(8,128)}, u32[]{:S(2)}) copy-start(f32[8,32,128]{2,1,0:T(8,128)} %param.53) | copy-start | bytes 393220
  15.6 25.7 %copy-start.1 = (f32[8,32,128]{2,1,0:T(8,128)S(1)}, f32[8,32,128]{2,1,0:T(8,128)}, u32[]{:S(2)}) copy-start(f32[8,32,128]{2,1,0:T(8,128)} %param.54) | copy-start | bytes 393220
  15.6 30.4 %copy-start.5 = (f32[8]{0:T(128)S(1)}, f32[8]{0:T(128)}, u32[]{:S(2)}) copy-start(f32[8]{0:T(128)} %param.57) | copy-start | bytes 100
  15.6 37.7 %copy-start.6 = (f32[8]{0:T(128)S(1)}, f32[8]{0:T(128)}, u32[]{:S(2)}) copy-start(f32[8]{0:T(128)} %param.56) | copy-start | bytes 100
  41.3 5.4 %collective-permute-start = (f32[3,1,32,128]{3,2,1,0:T(8,128)S(1)}, f32[3,1,32,128]{3,2,1,0:T(8,128)S(1)}, u32[]{:S(2)}, u32[]{:S(2)}) collective-permute-start(f32[3,1,32,128]{3,2,1,0:T(8,128)S(1)} %get-tuple-element.320), channel_id=1, source_target_pairs={{0,16},{1,17},{2,18},{3,19},{4,20},{5,21},{6,22},{7,23},{8,24},{9,... | collective-permute-start | bytes 147464 | tf_op jit(solution)/shard_map/ppermute | solution.py:14
  44.7 6.0 %collective-permute-start.1 = (f32[3,1,32,128]{3,2,1,0:T(8,128)S(1)}, f32[3,1,32,128]{3,2,1,0:T(8,128)S(1)}, u32[]{:S(2)}, u32[]{:S(2)}) collective-permute-start(f32[3,1,32,128]{3,2,1,0:T(8,128)S(1)} %get-tuple-element.321), channel_id=1, source_target_pairs={{16,0},{17,1},{18,2},{19,3},{20,4},{21,5},{22,6},{23,7},{24,8},{25... | collective-permute-start | bytes 147464 | tf_op jit(solution)/shard_map/ppermute | solution.py:17
  50.7 3.3 %collective-permute-start.2 = (f32[3,10,1,128]{3,2,1,0:T(1,128)S(1)}, f32[3,10,1,128]{3,2,1,0:T(1,128)S(1)}, u32[]{:S(2)}, u32[]{:S(2)}) collective-permute-start(f32[3,10,1,128]{3,2,1,0:T(1,128)S(1)} %get-tuple-element.306), channel_id=1, source_target_pairs={{0,4},{4,8},{8,12},{1,5},{5,9},{9,13},{2,6},{6,10},{10,14},{3,7},{... | collective-permute-start | bytes 46088 | tf_op jit(solution)/shard_map/ppermute | solution.py:14
  52.0 4.8 %collective-permute-start.3 = (f32[3,10,1,128]{3,2,1,0:T(1,128)S(1)}, f32[3,10,1,128]{3,2,1,0:T(1,128)S(1)}, u32[]{:S(2)}, u32[]{:S(2)}) collective-permute-start(f32[3,10,1,128]{3,2,1,0:T(1,128)S(1)} %get-tuple-element.307), channel_id=1, source_target_pairs={{4,0},{8,4},{12,8},{5,1},{9,5},{13,9},{6,2},{10,6},{14,10},{7,3},{... | collective-permute-start | bytes 46088 | tf_op jit(solution)/shard_map/ppermute | solution.py:17
  57.4 7.8 %collective-permute-start.4 = (f32[3,10,34,1]{2,3,1,0:T(1,128)S(1)}, f32[3,10,34,1]{2,3,1,0:T(1,128)S(1)}, u32[]{:S(2)}, u32[]{:S(2)}) collective-permute-start(f32[3,10,34,1]{2,3,1,0:T(1,128)S(1)} %copy.31), channel_id=1, source_target_pairs={{0,1},{1,2},{2,3},{4,5},{5,6},{6,7},{8,9},{9,10},{10,11},{12,13},{... | collective-permute-start | bytes 12248 | tf_op jit(solution)/shard_map/ppermute | solution.py:14
  60.3 5.6 %collective-permute-start.5 = (f32[3,10,34,1]{2,3,1,0:T(1,128)S(1)}, f32[3,10,34,1]{2,3,1,0:T(1,128)S(1)}, u32[]{:S(2)}, u32[]{:S(2)}) collective-permute-start(f32[3,10,34,1]{2,3,1,0:T(1,128)S(1)} %copy.32), channel_id=1, source_target_pairs={{1,0},{2,1},{3,2},{5,4},{6,5},{7,6},{9,8},{10,9},{11,10},{13,12},{... | collective-permute-start | bytes 12248 | tf_op jit(solution)/shard_map/ppermute | solution.py:17
  79.7 3.2 %collective-permute-start.6 = (f32[2,1,32,128]{3,2,1,0:T(8,128)S(1)}, f32[2,1,32,128]{3,2,1,0:T(8,128)S(1)}, u32[]{:S(2)}, u32[]{:S(2)}) collective-permute-start(f32[2,1,32,128]{3,2,1,0:T(8,128)S(1)} %get-tuple-element.328), channel_id=1, source_target_pairs={{0,16},{1,17},{2,18},{3,19},{4,20},{5,21},{6,22},{7,23},{8,24},{9,... | collective-permute-start | bytes 98312 | tf_op jit(solution)/shard_map/ppermute | solution.py:14
  81.3 5.8 %collective-permute-start.7 = (f32[2,1,32,128]{3,2,1,0:T(8,128)S(1)}, f32[2,1,32,128]{3,2,1,0:T(8,128)S(1)}, u32[]{:S(2)}, u32[]{:S(2)}) collective-permute-start(f32[2,1,32,128]{3,2,1,0:T(8,128)S(1)} %get-tuple-element.329), channel_id=1, source_target_pairs={{16,0},{17,1},{18,2},{19,3},{20,4},{21,5},{22,6},{23,7},{24,8},{25... | collective-permute-start | bytes 98312 | tf_op jit(solution)/shard_map/ppermute | solution.py:17
  87.1 3.7 %collective-permute-start.8 = (f32[2,10,1,128]{3,2,1,0:T(1,128)S(1)}, f32[2,10,1,128]{3,2,1,0:T(1,128)S(1)}, u32[]{:S(2)}, u32[]{:S(2)}) collective-permute-start(f32[2,10,1,128]{3,2,1,0:T(1,128)S(1)} %get-tuple-element.324), channel_id=1, source_target_pairs={{0,4},{4,8},{8,12},{1,5},{5,9},{9,13},{2,6},{6,10},{10,14},{3,7},{... | collective-permute-start | bytes 30728 | tf_op jit(solution)/shard_map/ppermute | solution.py:14
  89.5 4.6 %collective-permute-start.9 = (f32[2,10,1,128]{3,2,1,0:T(1,128)S(1)}, f32[2,10,1,128]{3,2,1,0:T(1,128)S(1)}, u32[]{:S(2)}, u32[]{:S(2)}) collective-permute-start(f32[2,10,1,128]{3,2,1,0:T(1,128)S(1)} %get-tuple-element.325), channel_id=1, source_target_pairs={{4,0},{8,4},{12,8},{5,1},{9,5},{13,9},{6,2},{10,6},{14,10},{7,3},{... | collective-permute-start | bytes 30728 | tf_op jit(solution)/shard_map/ppermute | solution.py:17
  94.3 12.6 %collective-permute-start.10 = (f32[2,10,34,1]{3,2,1,0:T(8,128)S(1)}, f32[2,10,34,1]{3,2,1,0:T(8,128)S(1)}, u32[]{:S(2)}, u32[]{:S(2)}) collective-permute-start(f32[2,10,34,1]{3,2,1,0:T(8,128)S(1)} %get-tuple-element.318), channel_id=1, source_target_pairs={{0,1},{1,2},{2,3},{4,5},{5,6},{6,7},{8,9},{9,10},{10,11},{12,13},{... | collective-permute-start | bytes 8168 | tf_op jit(solution)/shard_map/ppermute | solution.py:14
  98.6 13.0 %collective-permute-start.11 = (f32[2,10,34,1]{3,2,1,0:T(8,128)S(1)}, f32[2,10,34,1]{3,2,1,0:T(8,128)S(1)}, u32[]{:S(2)}, u32[]{:S(2)}) collective-permute-start(f32[2,10,34,1]{3,2,1,0:T(8,128)S(1)} %get-tuple-element.319), channel_id=1, source_target_pairs={{1,0},{2,1},{3,2},{5,4},{6,5},{7,6},{9,8},{10,9},{11,10},{13,12},{... | collective-permute-start | bytes 8168 | tf_op jit(solution)/shard_map/ppermute | solution.py:17
  113.4 3.3 %collective-permute-start.12 = (f32[2,1,32,128]{3,2,1,0:T(8,128)S(1)}, f32[2,1,32,128]{3,2,1,0:T(8,128)S(1)}, u32[]{:S(2)}, u32[]{:S(2)}) collective-permute-start(f32[2,1,32,128]{3,2,1,0:T(8,128)S(1)} %get-tuple-element.326), channel_id=1, source_target_pairs={{0,16},{1,17},{2,18},{3,19},{4,20},{5,21},{6,22},{7,23},{8,24},{9,... | collective-permute-start | bytes 98312 | tf_op jit(solution)/shard_map/ppermute | solution.py:14
  115.0 5.9 %collective-permute-start.13 = (f32[2,1,32,128]{3,2,1,0:T(8,128)S(1)}, f32[2,1,32,128]{3,2,1,0:T(8,128)S(1)}, u32[]{:S(2)}, u32[]{:S(2)}) collective-permute-start(f32[2,1,32,128]{3,2,1,0:T(8,128)S(1)} %get-tuple-element.327), channel_id=1, source_target_pairs={{16,0},{17,1},{18,2},{19,3},{20,4},{21,5},{22,6},{23,7},{24,8},{25... | collective-permute-start | bytes 98312 | tf_op jit(solution)/shard_map/ppermute | solution.py:17
  120.9 3.1 %collective-permute-start.14 = (f32[2,10,1,128]{3,2,1,0:T(1,128)S(1)}, f32[2,10,1,128]{3,2,1,0:T(1,128)S(1)}, u32[]{:S(2)}, u32[]{:S(2)}) collective-permute-start(f32[2,10,1,128]{3,2,1,0:T(1,128)S(1)} %get-tuple-element.322), channel_id=1, source_target_pairs={{0,4},{4,8},{8,12},{1,5},{5,9},{9,13},{2,6},{6,10},{10,14},{3,7},{... | collective-permute-start | bytes 30728 | tf_op jit(solution)/shard_map/ppermute | solution.py:14
  122.7 3.2 %collective-permute-start.15 = (f32[2,10,1,128]{3,2,1,0:T(1,128)S(1)}, f32[2,10,1,128]{3,2,1,0:T(1,128)S(1)}, u32[]{:S(2)}, u32[]{:S(2)}) collective-permute-start(f32[2,10,1,128]{3,2,1,0:T(1,128)S(1)} %get-tuple-element.323), channel_id=1, source_target_pairs={{4,0},{8,4},{12,8},{5,1},{9,5},{13,9},{6,2},{10,6},{14,10},{7,3},{... | collective-permute-start | bytes 30728 | tf_op jit(solution)/shard_map/ppermute | solution.py:17
  126.2 10.7 %collective-permute-start.16 = (f32[2,10,34,1]{3,2,1,0:T(8,128)S(1)}, f32[2,10,34,1]{3,2,1,0:T(8,128)S(1)}, u32[]{:S(2)}, u32[]{:S(2)}) collective-permute-start(f32[2,10,34,1]{3,2,1,0:T(8,128)S(1)} %get-tuple-element.312), channel_id=1, source_target_pairs={{0,1},{1,2},{2,3},{4,5},{5,6},{6,7},{8,9},{9,10},{10,11},{12,13},{... | collective-permute-start | bytes 8168 | tf_op jit(solution)/shard_map/ppermute | solution.py:14
  128.6 13.0 %collective-permute-start.17 = (f32[2,10,34,1]{3,2,1,0:T(8,128)S(1)}, f32[2,10,34,1]{3,2,1,0:T(8,128)S(1)}, u32[]{:S(2)}, u32[]{:S(2)}) collective-permute-start(f32[2,10,34,1]{3,2,1,0:T(8,128)S(1)} %get-tuple-element.313), channel_id=1, source_target_pairs={{1,0},{2,1},{3,2},{5,4},{6,5},{7,6},{9,8},{10,9},{11,10},{13,12},{... | collective-permute-start | bytes 8168 | tf_op jit(solution)/shard_map/ppermute | solution.py:17
  144.4 3.0 %collective-permute-start.18 = (f32[1,32,128]{2,1,0:T(8,128)S(1)}, f32[1,32,128]{2,1,0:T(8,128)S(1)}, u32[]{:S(2)}, u32[]{:S(2)}) collective-permute-start(f32[1,32,128]{2,1,0:T(8,128)S(1)} %get-tuple-element.334), channel_id=1, source_target_pairs={{0,16},{1,17},{2,18},{3,19},{4,20},{5,21},{6,22},{7,23},{8,24},{9,... | collective-permute-start | bytes 49160 | tf_op jit(solution)/shard_map/ppermute | solution.py:14
  146.1 5.6 %collective-permute-start.19 = (f32[1,32,128]{2,1,0:T(8,128)S(1)}, f32[1,32,128]{2,1,0:T(8,128)S(1)}, u32[]{:S(2)}, u32[]{:S(2)}) collective-permute-start(f32[1,32,128]{2,1,0:T(8,128)S(1)} %get-tuple-element.335), channel_id=1, source_target_pairs={{16,0},{17,1},{18,2},{19,3},{20,4},{21,5},{22,6},{23,7},{24,8},{25... | collective-permute-start | bytes 49160 | tf_op jit(solution)/shard_map/ppermute | solution.py:17
  151.7 11.2 %collective-permute-start.20 = (f32[10,1,128]{2,1,0:T(1,128)S(1)}, f32[10,1,128]{2,1,0:T(1,128)S(1)}, u32[]{:S(2)}, u32[]{:S(2)}) collective-permute-start(f32[10,1,128]{2,1,0:T(1,128)S(1)} %get-tuple-element.332), channel_id=1, source_target_pairs={{0,4},{4,8},{8,12},{1,5},{5,9},{9,13},{2,6},{6,10},{10,14},{3,7},{... | collective-permute-start | bytes 15368 | tf_op jit(solution)/shard_map/ppermute | solution.py:14
  153.2 9.7 %collective-permute-start.21 = (f32[10,1,128]{2,1,0:T(1,128)S(1)}, f32[10,1,128]{2,1,0:T(1,128)S(1)}, u32[]{:S(2)}, u32[]{:S(2)}) collective-permute-start(f32[10,1,128]{2,1,0:T(1,128)S(1)} %get-tuple-element.333), channel_id=1, source_target_pairs={{4,0},{8,4},{12,8},{5,1},{9,5},{13,9},{6,2},{10,6},{14,10},{7,3},{... | collective-permute-start | bytes 15368 | tf_op jit(solution)/shard_map/ppermute | solution.py:17
  163.1 7.2 %collective-permute-start.22 = (f32[10,34,1]{2,1,0:T(8,128)S(1)}, f32[10,34,1]{2,1,0:T(8,128)S(1)}, u32[]{:S(2)}, u32[]{:S(2)}) collective-permute-start(f32[10,34,1]{2,1,0:T(8,128)S(1)} %get-tuple-element.330), channel_id=1, source_target_pairs={{0,1},{1,2},{2,3},{4,5},{5,6},{6,7},{8,9},{9,10},{10,11},{12,13},{... | collective-permute-start | bytes 4088 | tf_op jit(solution)/shard_map/ppermute | solution.py:14
  165.6 9.5 %collective-permute-start.23 = (f32[10,34,1]{2,1,0:T(8,128)S(1)}, f32[10,34,1]{2,1,0:T(8,128)S(1)}, u32[]{:S(2)}, u32[]{:S(2)}) collective-permute-start(f32[10,34,1]{2,1,0:T(8,128)S(1)} %get-tuple-element.331), channel_id=1, source_target_pairs={{1,0},{2,1},{3,2},{5,4},{6,5},{7,6},{9,8},{10,9},{11,10},{13,12},{... | collective-permute-start | bytes 4088 | tf_op jit(solution)/shard_map/ppermute | solution.py:17
  180.0 41.1 %copy-start.8 = (f32[9]{0:T(128)S(1)}, f32[9]{0:T(128)}, u32[]{:S(2)}) copy-start(f32[9]{0:T(128)} %constant.686.clone.1) | copy-start | bytes 112
  180.0 41.8 %copy-start.7 = (f32[9]{0:T(128)S(1)}, f32[9]{0:T(128)}, u32[]{:S(2)}) copy-start(f32[9]{0:T(128)} %constant.661.clone.1) | copy-start | bytes 112
  180.0 41.8 %copy-start.9 = (f32[9,1]{0,1:T(1,128)S(1)}, f32[9,1]{0,1:T(1,128)}, u32[]{:S(2)}) copy-start(f32[9,1]{0,1:T(1,128)} %constant.803) | copy-start | bytes 112
  (4 other events, 62.1 us)
where the time goes:
time: 262 us; the launch traced here: 260 us
  waiting for transfers between devices  61.3 us (23%)
  starting transfers between devices  48.7 us (19%)
  other arithmetic  43.5 us (17%)
  local copies, waits for them, and re-layouts  42.3 us (16%)
  blocking collectives  38.1 us (15%)
  between operations  15.9 us (6%)
  matrix products  10.1 us (4%)
    ppermute x12, waiting for transfers between devices, extended(): lax.ppermute(lax.slice_in_dim(block, 0, width, axis=dim), axis, backward)  39.2 us
    psum x1, blocking collectives, body(): gram = lax.psum(partial_gram, ('gx', 'gy', 'gz'))  38.1 us
    ppermute x12, starting transfers between devices, extended(): lax.ppermute(lax.slice_in_dim(block, block.shape[dim] - width, None, axis...  26.8 us
    gather x1, local copies, waits for them, and re-layouts, body(): incoming = jnp.take_along_axis(arrived, slot, axis=1)  25.6 us
    ppermute x12, waiting for transfers between devices, extended(): lax.ppermute(lax.slice_in_dim(block, block.shape[dim] - width, None, axis...  18.2 us
    ppermute x12, starting transfers between devices, extended(): lax.ppermute(lax.slice_in_dim(block, 0, width, axis=dim), axis, backward)  15.5 us
    add x2, other arithmetic, combine(): summed = summed + weights[position] * basis[position]  12.6 us
    mul x5, other arithmetic, operate(): result = capacity * values  7.02 us
  transfers between devices with their start and end apart: 25, of which 18 were waited for; matrix products, arithmetic and copies ran while one was open for 5% of the time, Pallas kernels for 0%

commit v1 on v0

--- a/solution.py
+++ b/solution.py
@@ -179,7 +179,8 @@
     basis = dir_terms + res_terms
     stacked = jnp.stack([term.reshape(-1) for term in basis])
     partial_gram = jnp.dot(stacked, stacked.T, precision=lax.Precision.HIGHEST)
-    gram = lax.psum(partial_gram, ("gx", "gy", "gz"))
+    parts = lax.all_gather(partial_gram, ("gx", "gy", "gz"), axis=0, tiled=False)
+    gram = parts.sum(axis=0)
     moved, residue, direct = coefficients(gram, center, half_width, STEPS)
     return (solution_in + combine(moved, basis), combine(residue, basis), combine(direct, basis))
 

time: 262 us -> 289 us (1.10)
  blocking collectives: 38.1 us -> 65.9 us
    all_gather x0 -> x1, blocking collectives: none -> 65.9 us  [body(): lax.all_gather(partial_gram, ('gx', 'gy', 'gz'), axis=0, tiled=False)]
    psum x1 -> x0, blocking collectives: 38.1 us -> none  [body(): gram = lax.psum(partial_gram, ('gx', 'gy', 'gz'))]
  transfers between devices with their start and end apart: 25 -> 25, of which waited for: 18 -> 18; matrix products, arithmetic and copies ran while one was open for 5% -> 4% of each run, Pallas kernels for 0% -> 0%
where the time goes in v1:
time: 289 us; the launch traced here: 288 us
  blocking collectives  65.9 us (23%)
  waiting for transfers between devices  61.3 us (21%)
  starting transfers between devices  48.7 us (17%)
  other arithmetic  43.6 us (15%)
  local copies, waits for them, and re-layouts  42.3 us (15%)
  between operations  16 us (6%)
  matrix products  10.1 us (3%)
    all_gather x1, blocking collectives, body(): lax.all_gather(partial_gram, ('gx', 'gy', 'gz'), axis=0, tiled=False)  65.9 us
    ppermute x12, waiting for transfers between devices, extended(): lax.ppermute(lax.slice_in_dim(block, 0, width, axis=dim), axis, backward)  39.2 us
    ppermute x12, starting transfers between devices, extended(): lax.ppermute(lax.slice_in_dim(block, block.shape[dim] - width, None, axis...  26.8 us
    gather x1, local copies, waits for them, and re-layouts, body(): incoming = jnp.take_along_axis(arrived, slot, axis=1)  25.6 us
    ppermute x12, waiting for transfers between devices, extended(): lax.ppermute(lax.slice_in_dim(block, block.shape[dim] - width, None, axis...  18.2 us
    ppermute x12, starting transfers between devices, extended(): lax.ppermute(lax.slice_in_dim(block, 0, width, axis=dim), axis, backward)  15.5 us
    add x2, other arithmetic, combine(): summed = summed + weights[position] * basis[position]  12.6 us
    mul x5, other arithmetic, operate(): result = capacity * values  7.02 us
  transfers between devices with their start and end apart: 25, of which 18 were waited for; matrix products, arithmetic and copies ran while one was open for 4% of the time, Pallas kernels for 0%

profile of v1, /device:TPU:0, one launch (start us, length us, event | category | flops | bytes accessed | tf_op | source)
XLA Modules:
  0.0 287.8 jit_solution(6593477849912700853)
XLA Ops:
  2.2 6.3 %all-to-all-start = ((f32[4,1,1024]{2,1,0:T(1,128)}), f32[4,1,1024]{2,1,0:T(1,128)S(1)}, u32[]{:S(2)}, u32[]{:S(2)}) async-start(f32[4,1,1024]{2,1,0:T(1,128)} %reshape.749), calls=%async_computation | async-start | bytes 32768 | tf_op jit(solution)/shard_map/all_to_all | solution.py:140
  10.2 3.9 %all-to-all-done = f32[4,1,1024]{2,1,0:T(1,128)S(1)} async-done(((f32[4,1,1024]{2,1,0:T(1,128)}), f32[4,1,1024]{2,1,0:T(1,128)S(1)}, u32[]{:S(2)}, u32[]{:S(2)}) %all-to-all-start) | async-done | bytes 16416 | tf_op jit(solution)/shard_map/all_to_all | solution.py:140
  15.6 25.6 %gather_fusion = f32[4096]{0:T(1024)S(1)} fusion(f32[32,128]{1,0:T(8,128)S(1)} %reshape.660, s32[4096]{0:T(1024)S(1)} %fusion.80), kind=kCustom, calls=%fused_computation | custom fusion | bytes 65536 | tf_op jit(solution)/shard_map/jit(take_along_axis)/gather | solution.py:153
  41.3 3.4 %collective-permute-start = (f32[3,1,32,128]{3,2,1,0:T(8,128)S(1)}, f32[3,1,32,128]{3,2,1,0:T(8,128)S(1)}, u32[]{:S(2)}, u32[]{:S(2)}) collective-permute-start(f32[3,1,32,128]{3,2,1,0:T(8,128)S(1)} %get-tuple-element.320), channel_id=1, source_target_pairs={{0,16},{1,17},{2,18},{3,19},{4,20},{5,21},{6,22},{7,23},{8,24},{9,... | collective-permute-start | bytes 147464 | tf_op jit(solution)/shard_map/ppermute | solution.py:14
  46.7 4.0 %collective-permute-done.1 = f32[3,1,32,128]{3,2,1,0:T(8,128)S(1)} collective-permute-done((f32[3,1,32,128]{3,2,1,0:T(8,128)S(1)}, f32[3,1,32,128]{3,2,1,0:T(8,128)S(1)}, u32[]{:S(2)}, u32[]{:S(2)}) %collective-permute-start.1) | collective-permute-done | bytes 49184 | tf_op jit(solution)/shard_map/ppermute | solution.py:17
  54.0 2.8 collective-permute-done.3
  57.4 2.6 collective-permute-start.4
  67.0 5.8 %bitcast_multiply_fusion.6 = (f32[10,34,130]{2,1,0:T(8,128)S(1)}, f32[1,10,34,130]{3,2,1,0:T(8,128)S(1)}, pred[1,10,34,130]{3,2,1,0:T(8,128)(4,1)S(1)}, pred[1,1...) fusion(f32[3,10,34,130]{3,2,1,0:T(8,128)S(1)} %pad_maximum_fusi, ...), kind=kLoop, calls=%fused_computation.86 | loop fusion | flops 1060800 | bytes 1060832 | tf_op jit(solution)/shard_map/mul | solution.py:40
  72.8 5.4 %add_add_fusion = f32[1,10,34,130]{3,2,1,0:T(8,128)S(1)} fusion(pred[1,10,34,130]{3,2,1,0:T(8,128)(4,1)S(1)} %get-tuple-element.283, pred[1,10,34,130]{3,2,1,0:T(8,128)(4,1)S(1)} %get-tuple-element.282, pred[1,10,34,130]{3,2,1,0:T(8,128)(4,1)S(1)} %get-tuple-element.281, pred[1,10,34,130]{3,2,1,0:T(8,128)(4,1)S(1)} %get-tuple-element.280, ...), kind=kLoop, calls=%fused_computation.87 | loop fusion | flops 663000 | bytes 530432 | tf_op jit(solution)/shard_map/add | solution.py:65
  82.8 4.2 %collective-permute-done.7 = f32[2,1,32,128]{3,2,1,0:T(8,128)S(1)} collective-permute-done((f32[2,1,32,128]{3,2,1,0:T(8,128)S(1)}, f32[2,1,32,128]{3,2,1,0:T(8,128)S(1)}, u32[]{:S(2)}, u32[]{:S(2)}) %collective-permute-start.7) | collective-permute-done | bytes 32800 | tf_op jit(solution)/shard_map/ppermute | solution.py:17
  87.1 2.4 collective-permute-start.8
  90.8 3.3 %collective-permute-done.9 = f32[2,10,1,128]{3,2,1,0:T(1,128)S(1)} collective-permute-done((f32[2,10,1,128]{3,2,1,0:T(1,128)S(1)}, f32[2,10,1,128]{3,2,1,0:T(1,128)S(1)}, u32[]{:S(2)}, u32[]{:S(2)}) %collective-permute-start.9) | collective-permute-done | bytes 10272 | tf_op jit(solution)/shard_map/ppermute | solution.py:17
  94.3 4.3 %collective-permute-start.10 = (f32[2,10,34,1]{3,2,1,0:T(8,128)S(1)}, f32[2,10,34,1]{3,2,1,0:T(8,128)S(1)}, u32[]{:S(2)}, u32[]{:S(2)}) collective-permute-start(f32[2,10,34,1]{3,2,1,0:T(8,128)S(1)} %get-tuple-element.318), channel_id=1, source_target_pairs={{0,1},{1,2},{2,3},{4,5},{5,6},{6,7},{8,9},{9,10},{10,11},{12,13},{... | collective-permute-start | bytes 8168 | tf_op jit(solution)/shard_map/ppermute | solution.py:14
  99.9 7.0 %collective-permute-done.10 = f32[2,10,34,1]{3,2,1,0:T(8,128)S(1)} collective-permute-done((f32[2,10,34,1]{3,2,1,0:T(8,128)S(1)}, f32[2,10,34,1]{3,2,1,0:T(8,128)S(1)}, u32[]{:S(2)}, u32[]{:S(2)}) %collective-permute-start.10) | collective-permute-done | bytes 2752 | tf_op jit(solution)/shard_map/ppermute | solution.py:14
  106.9 4.7 %collective-permute-done.11 = f32[2,10,34,1]{3,2,1,0:T(8,128)S(1)} collective-permute-done((f32[2,10,34,1]{3,2,1,0:T(8,128)S(1)}, f32[2,10,34,1]{3,2,1,0:T(8,128)S(1)}, u32[]{:S(2)}, u32[]{:S(2)}) %collective-permute-start.11) | collective-permute-done | bytes 2752 | tf_op jit(solution)/shard_map/ppermute | solution.py:17
  116.7 4.2 %collective-permute-done.13 = f32[2,1,32,128]{3,2,1,0:T(8,128)S(1)} collective-permute-done((f32[2,1,32,128]{3,2,1,0:T(8,128)S(1)}, f32[2,1,32,128]{3,2,1,0:T(8,128)S(1)}, u32[]{:S(2)}, u32[]{:S(2)}) %collective-permute-start.13) | collective-permute-done | bytes 32800 | tf_op jit(solution)/shard_map/ppermute | solution.py:17
  120.9 1.8 collective-permute-start.14
  124.0 1.9 collective-permute-done.15
  126.2 2.4 collective-permute-start.16
  129.9 7.0 %collective-permute-done.16 = f32[2,10,34,1]{3,2,1,0:T(8,128)S(1)} collective-permute-done((f32[2,10,34,1]{3,2,1,0:T(8,128)S(1)}, f32[2,10,34,1]{3,2,1,0:T(8,128)S(1)}, u32[]{:S(2)}, u32[]{:S(2)}) %collective-permute-start.16) | collective-permute-done | bytes 2752 | tf_op jit(solution)/shard_map/ppermute | solution.py:14
  136.9 4.7 %collective-permute-done.17 = f32[2,10,34,1]{3,2,1,0:T(8,128)S(1)} collective-permute-done((f32[2,10,34,1]{3,2,1,0:T(8,128)S(1)}, f32[2,10,34,1]{3,2,1,0:T(8,128)S(1)}, u32[]{:S(2)}, u32[]{:S(2)}) %collective-permute-start.17) | collective-permute-done | bytes 2752 | tf_op jit(solution)/shard_map/ppermute | solution.py:17
  147.5 4.2 %collective-permute-done.19 = f32[1,32,128]{2,1,0:T(8,128)S(1)} collective-permute-done((f32[1,32,128]{2,1,0:T(8,128)S(1)}, f32[1,32,128]{2,1,0:T(8,128)S(1)}, u32[]{:S(2)}, u32[]{:S(2)}) %collective-permute-start.19) | collective-permute-done | bytes 16416 | tf_op jit(solution)/shard_map/ppermute | solution.py:17
  156.1 1.9 dynamic-slice.147
  163.1 2.5 collective-permute-start.22
  167.0 3.3 %collective-permute-done.22 = f32[10,34,1]{2,1,0:T(8,128)S(1)} collective-permute-done((f32[10,34,1]{2,1,0:T(8,128)S(1)}, f32[10,34,1]{2,1,0:T(8,128)S(1)}, u32[]{:S(2)}, u32[]{:S(2)}) %collective-permute-start.22) | collective-permute-done | bytes 1392 | tf_op jit(solution)/shard_map/ppermute | solution.py:14
  170.3 4.7 %collective-permute-done.23 = f32[10,34,1]{2,1,0:T(8,128)S(1)} collective-permute-done((f32[10,34,1]{2,1,0:T(8,128)S(1)}, f32[10,34,1]{2,1,0:T(8,128)S(1)}, u32[]{:S(2)}, u32[]{:S(2)}) %collective-permute-start.23) | collective-permute-done | bytes 1392 | tf_op jit(solution)/shard_map/ppermute | solution.py:17
  178.1 1.9 stack.43
  180.0 2.9 %convolution_bitcast_fusion = f32[1,9,9]{2,1,0:T(8,128)S(1)} fusion(f32[9,32768]{1,0:T(8,128)S(1)} %stack.43), kind=kOutput, calls=%fused_computation.6 | convolution fusion | flops 31850496 | bytes 1179972 | tf_op jit(solution)/shard_map/dot_general | solution.py:181
  183.0 65.9 %all-gather.1 = f32[32,9,9]{2,1,0:T(8,128)S(1)} all-gather(f32[1,9,9]{2,1,0:T(8,128)S(1)} %convolution_bitcast_fusion), channel_id=2, replica_groups=mesh['gx'=2,'gy'=4,'gz'=4] {'gx','gy','gz'}, dimensions={0}, use_global_device_ids=true | all-gather | bytes 10692 | tf_op jit(solution)/shard_map/all_gather | solution.py:182
  268.8 6.2 %multiply_add_fusion = f32[8,32,128]{2,1,0:T(8,128)} fusion(f32[8,32,128]{2,1,0:T(8,128)S(1)} %fusion.54, f32[8,32,128]{2,1,0:T(8,128)S(1)} %fusion.66, f32[8,32,128]{2,1,0:T(8,128)S(1)} %get-tuple-element.383, f32[8,32,128]{2,1,0:T(8,128)S(1)} %fusion.78, f32[8,32,128]{2,1,0:T(8,128)S(1)} %fusion.58, f32[8,32,128]{2,1,0:T(8,128)S(1)} %fusion.62, ...), kind=kLoop, calls=%fused_computation.188 | loop fusion | flops 557056 | bytes 1310756 | tf_op jit(solution)/shard_map/add | solution.py:126
  275.0 6.4 %multiply_add_fusion.1 = f32[8,32,128]{2,1,0:T(8,128)} fusion(f32[8,32,128]{2,1,0:T(8,128)S(1)} %fusion.54, f32[8,32,128]{2,1,0:T(8,128)S(1)} %fusion.66, f32[8,32,128]{2,1,0:T(8,128)S(1)} %get-tuple-element.383, f32[8,32,128]{2,1,0:T(8,128)S(1)} %fusion.78, f32[8,32,128]{2,1,0:T(8,128)S(1)} %fusion.58, f32[8,32,128]{2,1,0:T(8,128)S(1)} %fusion.62, ...), kind=kLoop, calls=%fused_computation.189 | loop fusion | flops 557056 | bytes 1310756 | tf_op jit(solution)/shard_map/add | solution.py:126
  281.4 6.4 %add_add_fusion.2 = f32[8,32,128]{2,1,0:T(8,128)} fusion(f32[8,32,128]{2,1,0:T(8,128)S(1)} %copy-done.3, f32[8,32,128]{2,1,0:T(8,128)S(1)} %fusion.54, f32[8,32,128]{2,1,0:T(8,128)S(1)} %fusion.66, f32[8,32,128]{2,1,0:T(8,128)S(1)} %get-tuple-element.383, f32[8,32,128]{2,1,0:T(8,128)S(1)} %fusion.78, f32[8,32,128]{2,1,0:T(8,128)S(1)} %fusion.58, ...), kind=kLoop, calls=%fused_computation.190 | loop fusion | flops 589824 | bytes 1441828 | tf_op jit(solution)/shard_map/add | solution.py:185
  (162 shorter events, 57.8 us)
Async XLA Ops:
  2.2 11.9 %all-to-all-start = ((f32[4,1,1024]{2,1,0:T(1,128)}), f32[4,1,1024]{2,1,0:T(1,128)S(1)}, u32[]{:S(2)}, u32[]{:S(2)}) async-start(f32[4,1,1024]{2,1,0:T(1,128)} %reshape.749), calls=%async_computation | async-start | bytes 32768 | tf_op jit(solution)/shard_map/all_to_all | solution.py:140
  15.5 25.7 %copy-start = (f32[8,32,128]{2,1,0:T(8,128)S(1)}, f32[8,32,128]{2,1,0:T(8,128)}, u32[]{:S(2)}) copy-start(f32[8,32,128]{2,1,0:T(8,128)} %param.53) | copy-start | bytes 393220
  15.6 25.7 %copy-start.1 = (f32[8,32,128]{2,1,0:T(8,128)S(1)}, f32[8,32,128]{2,1,0:T(8,128)}, u32[]{:S(2)}) copy-start(f32[8,32,128]{2,1,0:T(8,128)} %param.54) | copy-start | bytes 393220
  15.6 30.4 %copy-start.5 = (f32[8]{0:T(128)S(1)}, f32[8]{0:T(128)}, u32[]{:S(2)}) copy-start(f32[8]{0:T(128)} %param.57) | copy-start | bytes 100
  15.6 37.7 %copy-start.6 = (f32[8]{0:T(128)S(1)}, f32[8]{0:T(128)}, u32[]{:S(2)}) copy-start(f32[8]{0:T(128)} %param.56) | copy-start | bytes 100
  41.3 5.4 %collective-permute-start = (f32[3,1,32,128]{3,2,1,0:T(8,128)S(1)}, f32[3,1,32,128]{3,2,1,0:T(8,128)S(1)}, u32[]{:S(2)}, u32[]{:S(2)}) collective-permute-start(f32[3,1,32,128]{3,2,1,0:T(8,128)S(1)} %get-tuple-element.320), channel_id=1, source_target_pairs={{0,16},{1,17},{2,18},{3,19},{4,20},{5,21},{6,22},{7,23},{8,24},{9,... | collective-permute-start | bytes 147464 | tf_op jit(solution)/shard_map/ppermute | solution.py:14
  44.7 6.0 %collective-permute-start.1 = (f32[3,1,32,128]{3,2,1,0:T(8,128)S(1)}, f32[3,1,32,128]{3,2,1,0:T(8,128)S(1)}, u32[]{:S(2)}, u32[]{:S(2)}) collective-permute-start(f32[3,1,32,128]{3,2,1,0:T(8,128)S(1)} %get-tuple-element.321), channel_id=1, source_target_pairs={{16,0},{17,1},{18,2},{19,3},{20,4},{21,5},{22,6},{23,7},{24,8},{25... | collective-permute-start | bytes 147464 | tf_op jit(solution)/shard_map/ppermute | solution.py:17
  50.7 3.3 %collective-permute-start.2 = (f32[3,10,1,128]{3,2,1,0:T(1,128)S(1)}, f32[3,10,1,128]{3,2,1,0:T(1,128)S(1)}, u32[]{:S(2)}, u32[]{:S(2)}) collective-permute-start(f32[3,10,1,128]{3,2,1,0:T(1,128)S(1)} %get-tuple-element.306), channel_id=1, source_target_pairs={{0,4},{4,8},{8,12},{1,5},{5,9},{9,13},{2,6},{6,10},{10,14},{3,7},{... | collective-permute-start | bytes 46088 | tf_op jit(solution)/shard_map/ppermute | solution.py:14
  52.0 4.8 %collective-permute-start.3 = (f32[3,10,1,128]{3,2,1,0:T(1,128)S(1)}, f32[3,10,1,128]{3,2,1,0:T(1,128)S(1)}, u32[]{:S(2)}, u32[]{:S(2)}) collective-permute-start(f32[3,10,1,128]{3,2,1,0:T(1,128)S(1)} %get-tuple-element.307), channel_id=1, source_target_pairs={{4,0},{8,4},{12,8},{5,1},{9,5},{13,9},{6,2},{10,6},{14,10},{7,3},{... | collective-permute-start | bytes 46088 | tf_op jit(solution)/shard_map/ppermute | solution.py:17
  57.4 7.8 %collective-permute-start.4 = (f32[3,10,34,1]{2,3,1,0:T(1,128)S(1)}, f32[3,10,34,1]{2,3,1,0:T(1,128)S(1)}, u32[]{:S(2)}, u32[]{:S(2)}) collective-permute-start(f32[3,10,34,1]{2,3,1,0:T(1,128)S(1)} %copy.31), channel_id=1, source_target_pairs={{0,1},{1,2},{2,3},{4,5},{5,6},{6,7},{8,9},{9,10},{10,11},{12,13},{... | collective-permute-start | bytes 12248 | tf_op jit(solution)/shard_map/ppermute | solution.py:14
  60.3 5.6 %collective-permute-start.5 = (f32[3,10,34,1]{2,3,1,0:T(1,128)S(1)}, f32[3,10,34,1]{2,3,1,0:T(1,128)S(1)}, u32[]{:S(2)}, u32[]{:S(2)}) collective-permute-start(f32[3,10,34,1]{2,3,1,0:T(1,128)S(1)} %copy.32), channel_id=1, source_target_pairs={{1,0},{2,1},{3,2},{5,4},{6,5},{7,6},{9,8},{10,9},{11,10},{13,12},{... | collective-permute-start | bytes 12248 | tf_op jit(solution)/shard_map/ppermute | solution.py:17
  79.7 3.2 %collective-permute-start.6 = (f32[2,1,32,128]{3,2,1,0:T(8,128)S(1)}, f32[2,1,32,128]{3,2,1,0:T(8,128)S(1)}, u32[]{:S(2)}, u32[]{:S(2)}) collective-permute-start(f32[2,1,32,128]{3,2,1,0:T(8,128)S(1)} %get-tuple-element.328), channel_id=1, source_target_pairs={{0,16},{1,17},{2,18},{3,19},{4,20},{5,21},{6,22},{7,23},{8,24},{9,... | collective-permute-start | bytes 98312 | tf_op jit(solution)/shard_map/ppermute | solution.py:14
  81.3 5.8 %collective-permute-start.7 = (f32[2,1,32,128]{3,2,1,0:T(8,128)S(1)}, f32[2,1,32,128]{3,2,1,0:T(8,128)S(1)}, u32[]{:S(2)}, u32[]{:S(2)}) collective-permute-start(f32[2,1,32,128]{3,2,1,0:T(8,128)S(1)} %get-tuple-element.329), channel_id=1, source_target_pairs={{16,0},{17,1},{18,2},{19,3},{20,4},{21,5},{22,6},{23,7},{24,8},{25... | collective-permute-start | bytes 98312 | tf_op jit(solution)/shard_map/ppermute | solution.py:17
  87.1 3.7 %collective-permute-start.8 = (f32[2,10,1,128]{3,2,1,0:T(1,128)S(1)}, f32[2,10,1,128]{3,2,1,0:T(1,128)S(1)}, u32[]{:S(2)}, u32[]{:S(2)}) collective-permute-start(f32[2,10,1,128]{3,2,1,0:T(1,128)S(1)} %get-tuple-element.324), channel_id=1, source_target_pairs={{0,4},{4,8},{8,12},{1,5},{5,9},{9,13},{2,6},{6,10},{10,14},{3,7},{... | collective-permute-start | bytes 30728 | tf_op jit(solution)/shard_map/ppermute | solution.py:14
  89.5 4.6 %collective-permute-start.9 = (f32[2,10,1,128]{3,2,1,0:T(1,128)S(1)}, f32[2,10,1,128]{3,2,1,0:T(1,128)S(1)}, u32[]{:S(2)}, u32[]{:S(2)}) collective-permute-start(f32[2,10,1,128]{3,2,1,0:T(1,128)S(1)} %get-tuple-element.325), channel_id=1, source_target_pairs={{4,0},{8,4},{12,8},{5,1},{9,5},{13,9},{6,2},{10,6},{14,10},{7,3},{... | collective-permute-start | bytes 30728 | tf_op jit(solution)/shard_map/ppermute | solution.py:17
  94.3 12.6 %collective-permute-start.10 = (f32[2,10,34,1]{3,2,1,0:T(8,128)S(1)}, f32[2,10,34,1]{3,2,1,0:T(8,128)S(1)}, u32[]{:S(2)}, u32[]{:S(2)}) collective-permute-start(f32[2,10,34,1]{3,2,1,0:T(8,128)S(1)} %get-tuple-element.318), channel_id=1, source_target_pairs={{0,1},{1,2},{2,3},{4,5},{5,6},{6,7},{8,9},{9,10},{10,11},{12,13},{... | collective-permute-start | bytes 8168 | tf_op jit(solution)/shard_map/ppermute | solution.py:14
  98.6 13.0 %collective-permute-start.11 = (f32[2,10,34,1]{3,2,1,0:T(8,128)S(1)}, f32[2,10,34,1]{3,2,1,0:T(8,128)S(1)}, u32[]{:S(2)}, u32[]{:S(2)}) collective-permute-start(f32[2,10,34,1]{3,2,1,0:T(8,128)S(1)} %get-tuple-element.319), channel_id=1, source_target_pairs={{1,0},{2,1},{3,2},{5,4},{6,5},{7,6},{9,8},{10,9},{11,10},{13,12},{... | collective-permute-start | bytes 8168 | tf_op jit(solution)/shard_map/ppermute | solution.py:17
  113.4 3.3 %collective-permute-start.12 = (f32[2,1,32,128]{3,2,1,0:T(8,128)S(1)}, f32[2,1,32,128]{3,2,1,0:T(8,128)S(1)}, u32[]{:S(2)}, u32[]{:S(2)}) collective-permute-start(f32[2,1,32,128]{3,2,1,0:T(8,128)S(1)} %get-tuple-element.326), channel_id=1, source_target_pairs={{0,16},{1,17},{2,18},{3,19},{4,20},{5,21},{6,22},{7,23},{8,24},{9,... | collective-permute-start | bytes 98312 | tf_op jit(solution)/shard_map/ppermute | solution.py:14
  115.0 5.9 %collective-permute-start.13 = (f32[2,1,32,128]{3,2,1,0:T(8,128)S(1)}, f32[2,1,32,128]{3,2,1,0:T(8,128)S(1)}, u32[]{:S(2)}, u32[]{:S(2)}) collective-permute-start(f32[2,1,32,128]{3,2,1,0:T(8,128)S(1)} %get-tuple-element.327), channel_id=1, source_target_pairs={{16,0},{17,1},{18,2},{19,3},{20,4},{21,5},{22,6},{23,7},{24,8},{25... | collective-permute-start | bytes 98312 | tf_op jit(solution)/shard_map/ppermute | solution.py:17
  120.9 3.1 %collective-permute-start.14 = (f32[2,10,1,128]{3,2,1,0:T(1,128)S(1)}, f32[2,10,1,128]{3,2,1,0:T(1,128)S(1)}, u32[]{:S(2)}, u32[]{:S(2)}) collective-permute-start(f32[2,10,1,128]{3,2,1,0:T(1,128)S(1)} %get-tuple-element.322), channel_id=1, source_target_pairs={{0,4},{4,8},{8,12},{1,5},{5,9},{9,13},{2,6},{6,10},{10,14},{3,7},{... | collective-permute-start | bytes 30728 | tf_op jit(solution)/shard_map/ppermute | solution.py:14
  122.7 3.2 %collective-permute-start.15 = (f32[2,10,1,128]{3,2,1,0:T(1,128)S(1)}, f32[2,10,1,128]{3,2,1,0:T(1,128)S(1)}, u32[]{:S(2)}, u32[]{:S(2)}) collective-permute-start(f32[2,10,1,128]{3,2,1,0:T(1,128)S(1)} %get-tuple-element.323), channel_id=1, source_target_pairs={{4,0},{8,4},{12,8},{5,1},{9,5},{13,9},{6,2},{10,6},{14,10},{7,3},{... | collective-permute-start | bytes 30728 | tf_op jit(solution)/shard_map/ppermute | solution.py:17
  126.2 10.7 %collective-permute-start.16 = (f32[2,10,34,1]{3,2,1,0:T(8,128)S(1)}, f32[2,10,34,1]{3,2,1,0:T(8,128)S(1)}, u32[]{:S(2)}, u32[]{:S(2)}) collective-permute-start(f32[2,10,34,1]{3,2,1,0:T(8,128)S(1)} %get-tuple-element.312), channel_id=1, source_target_pairs={{0,1},{1,2},{2,3},{4,5},{5,6},{6,7},{8,9},{9,10},{10,11},{12,13},{... | collective-permute-start | bytes 8168 | tf_op jit(solution)/shard_map/ppermute | solution.py:14
  128.6 13.0 %collective-permute-start.17 = (f32[2,10,34,1]{3,2,1,0:T(8,128)S(1)}, f32[2,10,34,1]{3,2,1,0:T(8,128)S(1)}, u32[]{:S(2)}, u32[]{:S(2)}) collective-permute-start(f32[2,10,34,1]{3,2,1,0:T(8,128)S(1)} %get-tuple-element.313), channel_id=1, source_target_pairs={{1,0},{2,1},{3,2},{5,4},{6,5},{7,6},{9,8},{10,9},{11,10},{13,12},{... | collective-permute-start | bytes 8168 | tf_op jit(solution)/shard_map/ppermute | solution.py:17
  144.4 3.0 %collective-permute-start.18 = (f32[1,32,128]{2,1,0:T(8,128)S(1)}, f32[1,32,128]{2,1,0:T(8,128)S(1)}, u32[]{:S(2)}, u32[]{:S(2)}) collective-permute-start(f32[1,32,128]{2,1,0:T(8,128)S(1)} %get-tuple-element.334), channel_id=1, source_target_pairs={{0,16},{1,17},{2,18},{3,19},{4,20},{5,21},{6,22},{7,23},{8,24},{9,... | collective-permute-start | bytes 49160 | tf_op jit(solution)/shard_map/ppermute | solution.py:14
  146.1 5.6 %collective-permute-start.19 = (f32[1,32,128]{2,1,0:T(8,128)S(1)}, f32[1,32,128]{2,1,0:T(8,128)S(1)}, u32[]{:S(2)}, u32[]{:S(2)}) collective-permute-start(f32[1,32,128]{2,1,0:T(8,128)S(1)} %get-tuple-element.335), channel_id=1, source_target_pairs={{16,0},{17,1},{18,2},{19,3},{20,4},{21,5},{22,6},{23,7},{24,8},{25... | collective-permute-start | bytes 49160 | tf_op jit(solution)/shard_map/ppermute | solution.py:17
  151.7 11.2 %collective-permute-start.20 = (f32[10,1,128]{2,1,0:T(1,128)S(1)}, f32[10,1,128]{2,1,0:T(1,128)S(1)}, u32[]{:S(2)}, u32[]{:S(2)}) collective-permute-start(f32[10,1,128]{2,1,0:T(1,128)S(1)} %get-tuple-element.332), channel_id=1, source_target_pairs={{0,4},{4,8},{8,12},{1,5},{5,9},{9,13},{2,6},{6,10},{10,14},{3,7},{... | collective-permute-start | bytes 15368 | tf_op jit(solution)/shard_map/ppermute | solution.py:14
  153.2 9.7 %collective-permute-start.21 = (f32[10,1,128]{2,1,0:T(1,128)S(1)}, f32[10,1,128]{2,1,0:T(1,128)S(1)}, u32[]{:S(2)}, u32[]{:S(2)}) collective-permute-start(f32[10,1,128]{2,1,0:T(1,128)S(1)} %get-tuple-element.333), channel_id=1, source_target_pairs={{4,0},{8,4},{12,8},{5,1},{9,5},{13,9},{6,2},{10,6},{14,10},{7,3},{... | collective-permute-start | bytes 15368 | tf_op jit(solution)/shard_map/ppermute | solution.py:17
  163.1 7.2 %collective-permute-start.22 = (f32[10,34,1]{2,1,0:T(8,128)S(1)}, f32[10,34,1]{2,1,0:T(8,128)S(1)}, u32[]{:S(2)}, u32[]{:S(2)}) collective-permute-start(f32[10,34,1]{2,1,0:T(8,128)S(1)} %get-tuple-element.330), channel_id=1, source_target_pairs={{0,1},{1,2},{2,3},{4,5},{5,6},{6,7},{8,9},{9,10},{10,11},{12,13},{... | collective-permute-start | bytes 4088 | tf_op jit(solution)/shard_map/ppermute | solution.py:14
  165.6 9.5 %collective-permute-start.23 = (f32[10,34,1]{2,1,0:T(8,128)S(1)}, f32[10,34,1]{2,1,0:T(8,128)S(1)}, u32[]{:S(2)}, u32[]{:S(2)}) collective-permute-start(f32[10,34,1]{2,1,0:T(8,128)S(1)} %get-tuple-element.331), channel_id=1, source_target_pairs={{1,0},{2,1},{3,2},{5,4},{6,5},{7,6},{9,8},{10,9},{11,10},{13,12},{... | collective-permute-start | bytes 4088 | tf_op jit(solution)/shard_map/ppermute | solution.py:17
  180.0 68.9 %copy-start.8 = (f32[9]{0:T(128)S(1)}, f32[9]{0:T(128)}, u32[]{:S(2)}) copy-start(f32[9]{0:T(128)} %constant.686.clone.1) | copy-start | bytes 112
  180.0 69.6 %copy-start.7 = (f32[9]{0:T(128)S(1)}, f32[9]{0:T(128)}, u32[]{:S(2)}) copy-start(f32[9]{0:T(128)} %constant.661.clone.1) | copy-start | bytes 112
  180.0 69.6 %copy-start.9 = (f32[9,1]{0,1:T(1,128)S(1)}, f32[9,1]{0,1:T(1,128)}, u32[]{:S(2)}) copy-start(f32[9,1]{0,1:T(1,128)} %constant.803) | copy-start | bytes 112
  (4 other events, 62.1 us)
